TPU v7x, 32 devices: a whole 2x2x4 slice. The times are simulated.
32 devices in a mesh: chan: 4 (over y, x), space: 4 (over z), rep: 2 (over core).
Axes of the slice: x: 2, y: 2, z: 4, core: 2. Of those that a mesh axis runs over, the one named last changes fastest.
Arguments:
- inputs: bfloat16 [2, 2, 16, 512, 128], P('rep', None, 'space', 'chan'), may hold values from -6 to 6
- grad_out: bfloat16 [2, 2, 16, 512, 128], P('rep', None, 'space', 'chan'), may hold values from -6 to 6
- weight: bfloat16 [3, 3, 3, 512, 512], P(None, None, None, 'chan'), may hold values from -0.0546875 to 0.0546875
Outputs:
- grad_in: bfloat16 [2, 2, 16, 512, 128], P('rep', None, 'space', 'chan')
- grad_weight: float32 [3, 3, 3, 512, 512], P(None, None, None, ('chan', 'rep'))
All inputs are finite; a program needn't handle non-finite values.
Results may differ from a plain program's by a relative error of at most 0.0031.
Values may be sent and summed in bfloat16 or wider, within the bound.
A program may use at most 64 MiB of HBM per device.

v0:
```python
import jax
import jax.numpy as jnp
from jax import lax
from jax.sharding import PartitionSpec as P


def with_halo(cells, sides, width):
    for axis, dim in sides:
        count = lax.axis_size(axis)
        ends = count - 1
        head = lax.slice_in_dim(cells, 0, width, axis=dim)
        tail = lax.slice_in_dim(cells, cells.shape[dim] - width, cells.shape[dim], axis=dim)
        cells = jnp.concatenate(
            [
                lax.ppermute(tail, axis, [(i, (i + 1) % count) for i in range(ends)]),
                cells,
                lax.ppermute(head, axis, [((i + 1) % count, i) for i in range(ends)]),
            ],
            axis=dim,
        )
    return cells


def silu_slope(values):
    logistic = jax.nn.sigmoid(values)
    return logistic * (1.0 + values * (1.0 - logistic))


def tap_windows(padded, frame_count, row_count, col_count):
    windows = []
    for frame_tap in range(3):
        for row_tap in range(3):
            for col_tap in range(3):
                windows.append(
                    padded[
                        :,
                        2 - frame_tap : 2 - frame_tap + frame_count,
                        2 - row_tap : 2 - row_tap + row_count,
                        :,
                        2 - col_tap : 2 - col_tap + col_count,
                    ]
                )
    return jnp.concatenate(windows, axis=3)


def on_device(inputs, grad_out, weight):
    clip_count, frame_count, row_count, in_part, col_count = inputs.shape
    out_part = grad_out.shape[3]
    gathered = lax.all_gather(inputs, "chan", axis=3, tiled=True)
    activated = jax.nn.silu(gathered.astype(jnp.float32)).astype(jnp.bfloat16)
    in_width = activated.shape[3]
    grad_rim = with_halo(grad_out, (("space", 2),), 1)
    grad_pad = jnp.pad(grad_rim, ((0, 0), (0, 2), (0, 0), (0, 0), (1, 1)))
    stacked = tap_windows(grad_pad, frame_count, row_count, col_count)
    local_flat = jnp.einsum(
        "cthkw,cthiw->ki", stacked, activated, preferred_element_type=jnp.float32
    )
    local_weight = local_flat.reshape(3, 3, 3, out_part, in_width)
    clip_summed = lax.psum_scatter(local_weight, "rep", scatter_dimension=3, tiled=True)
    summed = lax.psum(clip_summed, "space")
    grad_weight = summed * (1.0 / 256.0)
    flat_kernel = weight.reshape(27 * out_part, weight.shape[4])
    partial_value = jnp.einsum(
        "cthkw,ki->cthiw", stacked, flat_kernel, preferred_element_type=jnp.float32
    )
    active_grad = lax.psum_scatter(partial_value, "chan", scatter_dimension=3, tiled=True)
    grad_in = (active_grad * silu_slope(inputs.astype(jnp.float32))).astype(jnp.bfloat16)
    return (grad_in, grad_weight)


def solution(mesh):
    return jax.shard_map(
        on_device,
        mesh=mesh,
        in_specs=(
            P("rep", None, "space", "chan", None),
            P("rep", None, "space", "chan", None),
            P(None, None, None, "chan", None),
        ),
        out_specs=(
            P("rep", None, "space", "chan", None),
            P(None, None, None, ("chan", "rep"), None),
        ),
        check_vma=False,
    )
```

profile of v0, /device:TPU:0, one launch (start us, length us, event | category | flops | bytes accessed | tf_op | source)
XLA Modules:
  0.0 258.9 jit_solution(6788880601391279087)
XLA Ops:
  7.2 1.9 copy.15
  9.2 1.5 fusion.32
  10.7 1.3 collective-permute-start.1
  12.0 6.2 %collective-permute-start = (bf16[1,2,1,128,128]{3,4,2,1,0:T(8,128)(2,1)}, bf16[1,2,1,128,128]{3,4,2,1,0:T(8,128)(2,1)}, u32[]{:S(2)}, u32[]{:S(2)}) collective-permute-start(bf16[1,2,1,128,128]{3,4,2,1,0:T(8,128)(2,1)} %get-tuple-element.6), channel_id=1, source_target_pairs={{0,2},{2,4},{4,6},{1,3},{3,5},{5,7},{8,10},{10,12},{12,14},{9,11},... | collective-permute-start | bytes 196616 | tf_op jit(solution)/shard_map/ppermute | solution.py:15
  18.2 0.0 reduce-scatter.5.cloned.1.call-start
  18.3 0.1 broadcast_dynamic-update-slice_fusion.6
  18.4 0.1 broadcast_dynamic-update-slice_fusion.5
  18.5 0.1 broadcast_dynamic-update-slice_fusion.4
  18.6 0.1 broadcast_dynamic-update-slice_fusion.3
  18.7 0.1 broadcast_dynamic-update-slice_fusion.2
  18.8 0.1 broadcast_dynamic-update-slice_fusion.1
  18.9 0.1 broadcast_dynamic-update-slice_fusion
  19.0 0.1 broadcast_dynamic-update-slice_fusion.8
  19.1 0.6 collective-permute-done
  19.7 1.2 fusion.20
  20.9 0.1 slice_dynamic-update-slice_fusion.14
  21.0 0.1 slice_dynamic-update-slice_fusion.13
  21.2 0.1 slice_dynamic-update-slice_fusion.12
  21.2 0.1 slice_dynamic-update-slice_fusion.11
  21.3 0.1 slice_dynamic-update-slice_fusion.10
  21.5 0.1 slice_dynamic-update-slice_fusion.9
  21.6 0.1 slice_dynamic-update-slice_fusion.8
  21.7 0.1 slice_dynamic-update-slice_fusion.7
  21.8 0.1 slice_dynamic-update-slice_fusion.6
  21.9 0.1 slice_dynamic-update-slice_fusion.5
  22.0 0.9 fusion.31
  22.9 0.1 slice_dynamic-update-slice_fusion.4
  23.0 0.1 slice_dynamic-update-slice_fusion.3
  23.1 0.1 constant_dynamic-update-slice_fusion
  23.2 0.1 slice_dynamic-update-slice_fusion.2
  23.3 0.1 slice_dynamic-update-slice_fusion.1
  23.4 0.9 fusion.30
  24.3 0.1 slice_dynamic-update-slice_fusion
  24.4 2.9 %copy-done.2 = bf16[1,2,4,3456,128]{3,4,2,1,0:T(8,128)(2,1)} copy-done((bf16[1,2,4,3456,128]{3,4,2,1,0:T(8,128)(2,1)}, bf16[1,2,4,3456,128]{3,4,2,1,0:T(8,128)(2,1)S(1)}, u32[]{:S(2)}) %copy-start.2) | copy-done | bytes 7077912
  27.3 10.2 %copy.22 = bf16[3456,4,2,128]{3,0,2,1:T(8,128)(2,1)} copy(bf16[3456,4,2,128]{0,3,1,2:T(8,128)(2,1)} %bitcast.31) | data formatting | bytes 14155776 | tf_op jit(solution)/shard_map/cthkw,cthiw->ki/dot_general | solution.py:55
  37.5 8.1 %all-gather.2.cloned.1.call-done = bf16[1,2,4,512,128]{4,3,2,1,0:T(8,128)(2,1)} async-done(((bf16[1,2,4,128,128]{4,3,2,1,0:T(8,128)(2,1)}), bf16[1,2,4,512,128]{4,3,2,1,0:T(8,128)(2,1)}) %all-gather.2.cloned.1.call-update) | async-done | bytes 1048592 | tf_op jit(solution)/shard_map/all_gather | solution.py:49
  45.6 6.6 %fusion = f32[3,3,3,128,512,1,1]{4,3,0,1,2,6,5:T(8,128)S(1)} fusion(bf16[3,3,3,128,4,2,128]{6,3,2,1,0,5,4:T(8,128)(2,1)} %bitcast.32, bf16[1,2,4,512,128]{4,3,2,1,0:T(8,128)(2,1)} %all-gather.2.cloned.1.call-done), kind=kOutput, calls=%fused_computation | convolution fusion | flops 3627024384 | bytes 15204352 | tf_op jit(solution)/shard_map/cthkw,cthiw->ki/dot_general | solution.py:55
  52.3 3.7 %copy.38 = f32[3,3,3,128,512,1,1]{4,3,2,1,0,5,6:T(8,128)} copy(f32[3,3,3,128,512,1,1]{4,3,0,1,2,6,5:T(8,128)S(1)} %fusion) | data formatting | bytes 14155776 | tf_op jit(solution)/shard_map/cthkw,cthiw->ki/dot_general | solution.py:55
  56.0 0.0 reduce-scatter.3.cloned.1.call-start
  56.1 7.5 %fusion.13 = f32[1,2,4,512,128]{3,4,2,1,0:T(8,128)} fusion(bf16[3456,512,1,1]{1,0,3,2:T(8,128)(2,1)S(1)} %bitcast.29, bf16[1,2,4,3456,128]{3,4,2,1,0:T(8,128)(2,1)} %copy-done.2), kind=kOutput, calls=%fused_computation.20 | convolution fusion | flops 3623878656 | bytes 12713984 | tf_op jit(solution)/shard_map/cthkw,ki->cthiw/dot_general | solution.py:63
  63.7 0.0 all-reduce.3.cloned.1.call-start
  63.7 7.9 %reduce-scatter.5.cloned.1.call-done = f32[3,3,3,64,512]{4,3,2,1,0:T(8,128)} async-done(((f32[3,3,3,128,512]{4,3,2,1,0:T(8,128)}), f32[3,3,3,64,512]{4,3,2,1,0:T(8,128)}) %reduce-scatter.5.cloned.1.call-update) | async-done | bytes 3538960 | tf_op jit(solution)/shard_map/reduce_scatter | solution.py:59
  71.7 1.8 copy.21
  73.5 38.5 %reduce-scatter.3.cloned.1.call-done = f32[1,2,4,128,128]{3,4,2,1,0:T(8,128)} async-done(((f32[1,2,4,512,128]{3,4,2,1,0:T(8,128)}), f32[1,2,4,128,128]{3,4,2,1,0:T(8,128)}) %reduce-scatter.3.cloned.1.call-update) | async-done | bytes 524304 | tf_op jit(solution)/shard_map/reduce_scatter | solution.py:66
  111.9 2.0 fusion.29
  113.9 1.8 copy.25
  115.7 132.2 %all-reduce.3.cloned.1.call-done = f32[3,3,3,64,512]{4,3,2,1,0:T(8,128)} async-done(((f32[3,3,3,64,512]{4,3,2,1,0:T(8,128)}), f32[3,3,3,64,512]{4,3,2,1,0:T(8,128)}) %all-reduce.3.cloned.1.call-update) | async-done | bytes 3538960 | tf_op jit(solution)/shard_map/psum | solution.py:60
  248.0 4.4 %broadcast_multiply_fusion = f32[3,3,3,64,512]{4,3,2,1,0:T(8,128)} fusion(f32[3,3,3,64,512]{4,3,2,1,0:T(8,128)} %all-reduce.3.cloned.1.call-done), kind=kLoop, calls=%fused_computation.13 | loop fusion | flops 884736 | bytes 7077888 | tf_op jit(solution)/shard_map/mul | solution.py:61
  (12 shorter events, 0.2 us)
Async XLA Ops:
  7.2 48.9 %copy-start = (bf16[3,3,3,128,512]{4,3,2,1,0:T(8,128)(2,1)S(1)}, bf16[3,3,3,128,512]{4,3,2,1,0:T(8,128)(2,1)}, u32[]{:S(2)}) copy-start(bf16[3,3,3,128,512]{4,3,2,1,0:T(8,128)(2,1)} %param.5) | copy-start | bytes 10616836
  7.2 38.5 %all-gather.2.cloned.1.call-start = ((), (), s32[]{:S(2)}) async-start(), calls=%async_computation.3 | async-start | bytes 1310720 | tf_op jit(solution)/shard_map/all_gather | solution.py:49
  10.7 8.5 %collective-permute-start.1 = (bf16[1,2,1,128,128]{3,4,2,1,0:T(8,128)(2,1)}, bf16[1,2,1,128,128]{3,4,2,1,0:T(8,128)(2,1)}, u32[]{:S(2)}, u32[]{:S(2)}) collective-permute-start(bf16[1,2,1,128,128]{3,4,2,1,0:T(8,128)(2,1)} %get-tuple-element.7), channel_id=1, source_target_pairs={{2,0},{4,2},{6,4},{3,1},{5,3},{7,5},{10,8},{12,10},{14,12},{11,9},... | collective-permute-start | bytes 196616 | tf_op jit(solution)/shard_map/ppermute | solution.py:17
  12.0 7.8 %collective-permute-start = (bf16[1,2,1,128,128]{3,4,2,1,0:T(8,128)(2,1)}, bf16[1,2,1,128,128]{3,4,2,1,0:T(8,128)(2,1)}, u32[]{:S(2)}, u32[]{:S(2)}) collective-permute-start(bf16[1,2,1,128,128]{3,4,2,1,0:T(8,128)(2,1)} %get-tuple-element.6), channel_id=1, source_target_pairs={{0,2},{2,4},{4,6},{1,3},{3,5},{5,7},{8,10},{10,12},{12,14},{9,11},... | collective-permute-start | bytes 196616 | tf_op jit(solution)/shard_map/ppermute | solution.py:15
  18.2 53.4 %reduce-scatter.5.cloned.1.call-start = ((), (), s32[]{:S(2)}) async-start(), calls=%async_computation.4 | async-start | bytes 10616832 | tf_op jit(solution)/shard_map/reduce_scatter | solution.py:59
  18.2 3.8 %copy-start.1 = (bf16[1,2,4,128,128]{3,4,2,1,0:T(8,128)(2,1)S(1)}, bf16[1,2,4,128,128]{3,4,2,1,0:T(8,128)(2,1)}, u32[]{:S(2)}) copy-start(bf16[1,2,4,128,128]{3,4,2,1,0:T(8,128)(2,1)} %copy.15) | copy-start | bytes 786436
  24.4 2.9 %copy-start.2 = (bf16[1,2,4,3456,128]{3,4,2,1,0:T(8,128)(2,1)}, bf16[1,2,4,3456,128]{3,4,2,1,0:T(8,128)(2,1)S(1)}, u32[]{:S(2)}) copy-start(bf16[1,2,4,3456,128]{3,4,2,1,0:T(8,128)(2,1)S(1)} %slice_dynamic-update-slice_fusion) | copy-start | bytes 21233668
  56.0 55.9 %reduce-scatter.3.cloned.1.call-start = ((), (), s32[]{:S(2)}) async-start(), calls=%async_computation.2 | async-start | bytes 2621440 | tf_op jit(solution)/shard_map/reduce_scatter | solution.py:66
  63.7 184.3 %all-reduce.3.cloned.1.call-start = ((), (), s32[]{:S(2)}) async-start(), calls=%async_computation.5 | async-start | bytes 7077888 | tf_op jit(solution)/shard_map/psum | solution.py:60
Sparse Core Ops, SparseCore 0:
  18.3 27.2 all-gather.1
  56.2 15.4 reduce-scatter.4
  75.5 36.4 reduce-scatter.2
  114.2 133.7 all-reduce.2
where the time goes:
time: 260 us; the launch traced here: 259 us
  waiting for transfers between devices  187 us (72%)
  local copies, waits for them, and re-layouts  26.3 us (10%)
  matrix products  14.2 us (5%)
  between operations  14 us (5%)
  other arithmetic  9.39 us (4%)
  starting transfers between devices  7.63 us (3%)
    psum x1, waiting for transfers between devices, on_device(): summed = lax.psum(clip_summed, 'space')  132 us
    reduce_scatter x1, waiting for transfers between devices, on_device(): lax.psum_scatter(partial_value, 'chan', scatter_dimension=3, tiled=True)  38.5 us
    dot_general x2, local copies, waits for them, and re-layouts, on_device(): jnp.einsum('cthkw,cthiw->ki', stacked, activated, preferred_element_type=...  14 us
    unnamed x33, local copies, waits for them, and re-layouts  10.7 us
    all_gather x1, waiting for transfers between devices, on_device(): gathered = lax.all_gather(inputs, 'chan', axis=3, tiled=True)  8.09 us
    reduce_scatter x1, waiting for transfers between devices, on_device(): lax.psum_scatter(local_weight, 'rep', scatter_dimension=3, tiled=True)  7.92 us
    dot_general x1, matrix products, on_device(): jnp.einsum('cthkw,ki->cthiw', stacked, flat_kernel, preferred_element_typ...  7.54 us
    dot_general x1, matrix products, on_device(): jnp.einsum('cthkw,cthiw->ki', stacked, activated, preferred_element_type=...  6.64 us
  transfers between devices with their start and end apart: 6, of which 5 were waited for; matrix products, arithmetic and copies ran while one was open for 11% of the time, Pallas kernels for 0%

commit v1 on v0

--- a/solution.py
+++ b/solution.py
@@ -57,7 +57,8 @@
     )
     local_weight = local_flat.reshape(3, 3, 3, out_part, in_width)
     clip_summed = lax.psum_scatter(local_weight, "rep", scatter_dimension=3, tiled=True)
-    summed = lax.psum(clip_summed, "space")
+    blocks = lax.all_gather(clip_summed, "space", axis=0, tiled=False)
+    summed = blocks.sum(axis=0)
     grad_weight = summed * (1.0 / 256.0)
     flat_kernel = weight.reshape(27 * out_part, weight.shape[4])
     partial_value = jnp.einsum(

time: 260 us -> 371 us (1.43)
  waiting for transfers between devices: 187 us -> 289 us
  other arithmetic: 9.39 us -> 16.7 us
    all_gather x0 -> x1, waiting for transfers between devices: none -> 242 us  [on_device(): blocks = lax.all_gather(clip_summed, 'space', axis=0, tiled=False)]
    psum x1 -> x0, waiting for transfers between devices: 132 us -> none  [on_device(): summed = lax.psum(clip_summed, 'space')]
    reduce_sum x0 -> x1, other arithmetic: none -> 9 us  [on_device(): summed = blocks.sum(axis=0)]
    all_gather x1, waiting for transfers between devices: 8.09 us -> 1.25 us  [on_device(): gathered = lax.all_gather(inputs, 'chan', axis=3, tiled=True)]
    reduce_scatter x1, waiting for transfers between devices: 38.5 us -> 33.5 us  [on_device(): lax.psum_scatter(partial_value, 'chan', scatter_dimension=3, tiled=True)]
    reduce_scatter x0 -> x1, local copies, waits for them, and re-layouts: none -> 4.39 us  [on_device(): lax.psum_scatter(local_weight, 'rep', scatter_dimension=3, tiled=True)]
    ppermute x1, waiting for transfers between devices: 0.01 us -> 3.97 us  [with_halo(): lax.ppermute(head, axis, [((i + 1) % count, i) for i in range(ends)])]
  transfers between devices with their start and end apart: 6 -> 6, of which waited for: 5 -> 5; matrix products, arithmetic and copies ran while one was open for 11% -> 9% of each run, Pallas kernels for 0% -> 0%
where the time goes in v1:
time: 371 us
  waiting for transfers between devices  289 us (78%)
  local copies, waits for them, and re-layouts  30 us (8%)
  other arithmetic  16.7 us (5%)
  matrix products  14.2 us (4%)
  between operations  14 us (4%)
  starting transfers between devices  6.38 us (2%)
    all_gather x1, waiting for transfers between devices, on_device(): blocks = lax.all_gather(clip_summed, 'space', axis=0, tiled=False)  242 us
    reduce_scatter x1, waiting for transfers between devices, on_device(): lax.psum_scatter(partial_value, 'chan', scatter_dimension=3, tiled=True)  33.5 us
    dot_general x2, local copies, waits for them, and re-layouts, on_device(): jnp.einsum('cthkw,cthiw->ki', stacked, activated, preferred_element_type=...  13.8 us
    unnamed x33, local copies, waits for them, and re-layouts  10.9 us
    reduce_sum x1, other arithmetic, on_device(): summed = blocks.sum(axis=0)  9 us
    reduce_scatter x1, waiting for transfers between devices, on_device(): lax.psum_scatter(local_weight, 'rep', scatter_dimension=3, tiled=True)  7.9 us
    dot_general x1, matrix products, on_device(): jnp.einsum('cthkw,ki->cthiw', stacked, flat_kernel, preferred_element_typ...  7.57 us
  transfers between devices with their start and end apart: 6, of which 5 were waited for; matrix products, arithmetic and copies ran while one was open for 9% of the time, Pallas kernels for 0%

profile of v1, /device:TPU:0, one launch (start us, length us, event | category | flops | bytes accessed | tf_op | source)
XLA Modules:
  0.0 370.8 jit_solution(9080213999918443456)
XLA Ops:
  7.2 0.7 all-gather.4.cloned.1.call-update
  8.0 2.1 copy.26
  10.0 0.9 fusion.31
  11.0 4.9 %collective-permute-start = (bf16[1,2,1,128,128]{3,4,2,1,0:T(8,128)(2,1)S(1)}, bf16[1,2,1,128,128]{3,4,2,1,0:T(8,128)(2,1)S(1)}, u32[]{:S(2)}, u32[]{:S(2)}) collective-permute-start(bf16[1,2,1,128,128]{3,4,2,1,0:T(8,128)(2,1)S(1)} %get-tuple-element.8), channel_id=1, source_target_pairs={{0,2},{2,4},{4,6},{1,3},{3,5},{5,7},{8,10},{10,12},{12,14},{9,11},... | collective-permute-start | bytes 196616 | tf_op jit(solution)/shard_map/ppermute | solution.py:15
  15.9 1.3 collective-permute-start.1
  17.2 0.1 broadcast_dynamic-update-slice_fusion.6
  17.3 0.1 broadcast_dynamic-update-slice_fusion.5
  17.4 0.1 broadcast_dynamic-update-slice_fusion.4
  17.6 0.1 broadcast_dynamic-update-slice_fusion.3
  17.7 0.1 broadcast_dynamic-update-slice_fusion.2
  17.8 0.1 broadcast_dynamic-update-slice_fusion.1
  17.9 0.1 broadcast_dynamic-update-slice_fusion
  18.0 0.1 broadcast_dynamic-update-slice_fusion.8
  18.1 4.0 %collective-permute-done.1 = bf16[1,2,1,128,128]{3,4,2,1,0:T(8,128)(2,1)S(1)} collective-permute-done((bf16[1,2,1,128,128]{3,4,2,1,0:T(8,128)(2,1)S(1)}, bf16[1,2,1,128,128]{3,4,2,1,0:T(8,128)(2,1)S(1)}, u32[]{:S(2)}, u32[]{:S(2)}) %collective-permute-start.1) | collective-permute-done | bytes 65568 | tf_op jit(solution)/shard_map/ppermute | solution.py:17
  22.1 1.1 fusion.19
  23.2 0.1 slice_dynamic-update-slice_fusion.14
  23.3 0.1 slice_dynamic-update-slice_fusion.13
  23.4 0.1 slice_dynamic-update-slice_fusion.12
  23.5 0.1 slice_dynamic-update-slice_fusion.11
  23.6 0.1 slice_dynamic-update-slice_fusion.10
  23.7 0.1 slice_dynamic-update-slice_fusion.9
  23.8 0.1 slice_dynamic-update-slice_fusion.8
  24.0 0.1 slice_dynamic-update-slice_fusion.7
  24.1 0.1 slice_dynamic-update-slice_fusion.6
  24.2 0.1 slice_dynamic-update-slice_fusion.5
  24.3 0.1 fusion.30
  24.4 0.1 slice_dynamic-update-slice_fusion.4
  24.4 0.1 slice_dynamic-update-slice_fusion.3
  24.6 0.1 constant_dynamic-update-slice_fusion
  24.6 0.1 slice_dynamic-update-slice_fusion.2
  24.7 0.1 slice_dynamic-update-slice_fusion.1
  24.8 0.1 fusion.29
  24.9 0.1 slice_dynamic-update-slice_fusion
  25.0 2.9 copy-done.2
  27.9 10.1 %copy.33 = bf16[3456,4,2,128]{3,0,2,1:T(8,128)(2,1)} copy(bf16[3456,4,2,128]{0,3,1,2:T(8,128)(2,1)} %bitcast.34) | data formatting | bytes 14155776 | tf_op jit(solution)/shard_map/cthkw,cthiw->ki/dot_general | solution.py:55
  38.0 1.3 all-gather.4.cloned.1.call-done
  39.2 6.6 %fusion.15 = f32[3,3,3,128,512,1,1]{4,3,2,1,0,6,5:T(8,128)S(1)} fusion(bf16[3,3,3,128,4,2,128]{6,3,2,1,0,5,4:T(8,128)(2,1)} %bitcast.35, bf16[1,2,4,512,128]{4,3,2,1,0:T(8,128)(2,1)} %all-gather.4.cloned.1.call-done), kind=kOutput, calls=%fused_computation.20 | convolution fusion | flops 3627024384 | bytes 15204352 | tf_op jit(solution)/shard_map/cthkw,cthiw->ki/dot_general | solution.py:55
  45.9 3.7 %copy.47 = f32[3,3,3,128,512,1,1]{4,3,0,1,2,5,6:T(8,128)} copy(f32[3,3,3,128,512,1,1]{4,3,2,1,0,6,5:T(8,128)S(1)} %fusion.15) | data formatting | bytes 14155776 | tf_op jit(solution)/shard_map/cthkw,cthiw->ki/dot_general | solution.py:55
  49.7 7.6 %fusion.11 = f32[1,2,4,512,128]{3,4,2,1,0:T(8,128)} fusion(bf16[3456,512,1,1]{1,0,3,2:T(8,128)(2,1)S(1)} %bitcast.31, bf16[1,2,4,3456,128]{3,4,2,1,0:T(8,128)(2,1)} %copy-done.2), kind=kOutput, calls=%fused_computation.18 | convolution fusion | flops 3623878656 | bytes 12713984 | tf_op jit(solution)/shard_map/cthkw,ki->cthiw/dot_general | solution.py:64
  57.3 7.9 %reduce-scatter.5.cloned.1.call-done = f32[3,3,3,64,512]{4,3,0,1,2:T(8,128)} async-done(((f32[3,3,3,128,512]{4,3,0,1,2:T(8,128)}), f32[3,3,3,64,512]{4,3,0,1,2:T(8,128)}) %reduce-scatter.5.cloned.1.call-update) | async-done | bytes 3538960 | tf_op jit(solution)/shard_map/reduce_scatter | solution.py:59
  65.2 4.4 %copy.36 = f32[3,3,3,64,512]{4,3,2,1,0:T(8,128)} copy(f32[3,3,3,64,512]{4,3,0,1,2:T(8,128)} %reduce-scatter.5.cloned.1.call-done) | data formatting | bytes 7077888 | tf_op jit(solution)/shard_map/reduce_scatter | solution.py:59
  69.6 1.8 copy.32
  71.4 33.5 %reduce-scatter.3.cloned.1.call-done = f32[1,2,4,128,128]{3,4,2,1,0:T(8,128)} async-done(((f32[1,2,4,512,128]{3,4,2,1,0:T(8,128)}), f32[1,2,4,128,128]{3,4,2,1,0:T(8,128)}) %reduce-scatter.3.cloned.1.call-update) | async-done | bytes 524304 | tf_op jit(solution)/shard_map/reduce_scatter | solution.py:67
  104.9 2.0 fusion.28
  106.9 1.8 copy.37
  108.7 242.1 %all-gather.6.cloned.1.call-done = f32[12,3,3,64,512]{4,3,2,1,0:T(8,128)} async-done(((f32[3,3,3,64,512]{4,3,2,1,0:T(8,128)}), f32[12,3,3,64,512]{4,3,2,1,0:T(8,128)}) %all-gather.6.cloned.1.call-update) | async-done | bytes 14155792 | tf_op jit(solution)/shard_map/all_gather | solution.py:60
  350.8 9.0 %reduce_sum.9 = f32[3,3,3,64,512]{4,3,2,1,0:T(8,128)} reduce(f32[4,3,3,3,64,512]{5,4,3,2,1,0:T(8,128)} %bitcast.33, f32[]{:T(128)} %constant.3.clone.1), dimensions={0}, to_apply=%region_2.3 | reduce | flops 2654208 | bytes 17694724 | tf_op jit(solution)/shard_map/reduce_sum | solution.py:61
  359.9 4.4 %broadcast_multiply_fusion = f32[3,3,3,64,512]{4,3,2,1,0:T(8,128)} fusion(f32[3,3,3,64,512]{4,3,2,1,0:T(8,128)} %reduce_sum.9), kind=kLoop, calls=%fused_computation.11 | loop fusion | flops 884736 | bytes 7077888 | tf_op jit(solution)/shard_map/mul | solution.py:62
  (14 shorter events, 0.3 us)
Async XLA Ops:
  7.2 42.5 %copy-start = (bf16[3,3,3,128,512]{4,3,2,1,0:T(8,128)(2,1)S(1)}, bf16[3,3,3,128,512]{4,3,2,1,0:T(8,128)(2,1)}, u32[]{:S(2)}) copy-start(bf16[3,3,3,128,512]{4,3,2,1,0:T(8,128)(2,1)} %param.5) | copy-start | bytes 10616836
  7.2 32.0 %all-gather.4.cloned.1.call-start = ((), (), s32[]{:S(2)}) async-start(), calls=%async_computation.3 | async-start | bytes 1310720 | tf_op jit(solution)/shard_map/all_gather | solution.py:49
  7.9 57.3 %reduce-scatter.5.cloned.1.call-start = ((), (), s32[]{:S(2)}) async-start(), calls=%async_computation.4 | async-start | bytes 10616832 | tf_op jit(solution)/shard_map/reduce_scatter | solution.py:59
  10.0 14.2 %copy-start.1 = (bf16[1,2,4,128,128]{3,4,2,1,0:T(8,128)(2,1)S(1)}, bf16[1,2,4,128,128]{3,4,2,1,0:T(8,128)(2,1)}, u32[]{:S(2)}) copy-start(bf16[1,2,4,128,128]{3,4,2,1,0:T(8,128)(2,1)} %copy.26) | copy-start | bytes 786436
  11.0 7.1 %collective-permute-start = (bf16[1,2,1,128,128]{3,4,2,1,0:T(8,128)(2,1)S(1)}, bf16[1,2,1,128,128]{3,4,2,1,0:T(8,128)(2,1)S(1)}, u32[]{:S(2)}, u32[]{:S(2)}) collective-permute-start(bf16[1,2,1,128,128]{3,4,2,1,0:T(8,128)(2,1)S(1)} %get-tuple-element.8), channel_id=1, source_target_pairs={{0,2},{2,4},{4,6},{1,3},{3,5},{5,7},{8,10},{10,12},{12,14},{9,11},... | collective-permute-start | bytes 196616 | tf_op jit(solution)/shard_map/ppermute | solution.py:15
  15.9 6.2 %collective-permute-start.1 = (bf16[1,2,1,128,128]{3,4,2,1,0:T(8,128)(2,1)S(1)}, bf16[1,2,1,128,128]{3,4,2,1,0:T(8,128)(2,1)S(1)}, u32[]{:S(2)}, u32[]{:S(2)}) collective-permute-start(bf16[1,2,1,128,128]{3,4,2,1,0:T(8,128)(2,1)S(1)} %get-tuple-element.9), channel_id=1, source_target_pairs={{2,0},{4,2},{6,4},{3,1},{5,3},{7,5},{10,8},{12,10},{14,12},{11,9},... | collective-permute-start | bytes 196616 | tf_op jit(solution)/shard_map/ppermute | solution.py:17
  25.0 2.9 copy-start.2
  49.6 55.3 %reduce-scatter.3.cloned.1.call-start = ((), (), s32[]{:S(2)}) async-start(), calls=%async_computation.2 | async-start | bytes 2621440 | tf_op jit(solution)/shard_map/reduce_scatter | solution.py:67
  57.3 293.6 %all-gather.6.cloned.1.call-start = ((), (), s32[]{:S(2)}) async-start(), calls=%async_computation.5 | async-start | bytes 17694720 | tf_op jit(solution)/shard_map/all_gather | solution.py:60
Sparse Core Ops, SparseCore 0:
  9.9 29.3 all-gather.3
  49.8 15.4 reduce-scatter.4
  68.5 36.3 reduce-scatter.2
  106.9 243.9 all-gather.5
